TPU v7x, 256 devices: a whole 4x4x8 slice. The times are simulated.
256 devices in a mesh: snap: 16 (over z, x_hi), mesh: 16 (over x_lo, y, core).
Axes of the slice: x: 4 (x_hi: 2, x_lo: 2; x = x_hi * 2 + x_lo), y: 4, z: 8, core: 2. Of those that a mesh axis runs over, the one named last changes fastest.
Arguments:
- snapshots: float32 [49152, 2048], P('mesh', 'snap'), may hold values from -6 to 6
- region_ids: int32 [96, 512], P('mesh'), may hold values from 0 to 7
- conductivity: float32 [8], replicated, may hold values from 0.2 to 5
Outputs:
- gram: float32 [2048, 2048], P('snap', 'mesh')
All inputs are finite; a program needn't handle non-finite values.
Results may differ from a plain program's by a relative error of at most 0.0003.
Values sent between devices are 32-bit elements; how exact they have to be, the bound alone decides.
A program may use at most 128 MiB of HBM per device.

v0:
```python
import math
import jax
import jax.numpy as jnp
from jax import lax
from jax.sharding import PartitionSpec as P


def passed_along(value, axis, steps):
    count = lax.axis_size(axis)
    first, last = (max(0, -steps), min(count, count - steps))
    return lax.ppermute(value, axis, [(source, source + steps) for source in range(first, last)])


def weights_of(region_ids, conductivity):
    table = jnp.arange(conductivity.shape[0], dtype=jnp.int32)
    picked = jnp.where(
        region_ids[:, :, None] == table[None, None, :],
        conductivity[None, None, :],
        jnp.zeros((), conductivity.dtype),
    )
    return jnp.sum(picked, axis=-1) / 36.0


def element_terms(field, below, weight):
    lower = jnp.concatenate([field, below[None]], 0)
    padded = jnp.pad(lower, ((0, 0), (0, 1), (0, 0)))
    corner_a = padded[:-1, :-1]
    corner_b = padded[:-1, 1:]
    corner_e = padded[1:, :-1]
    corner_d = padded[1:, 1:]
    scaled = weight[:, :, None]
    to_a = scaled * (4.0 * corner_a + 2.0 * corner_b + 2.0 * corner_e + corner_d)
    to_b = scaled * (2.0 * corner_a + 4.0 * corner_b + corner_e + 2.0 * corner_d)
    to_e = scaled * (2.0 * corner_a + corner_b + 4.0 * corner_e + 2.0 * corner_d)
    to_d = scaled * (corner_a + 2.0 * corner_b + 2.0 * corner_e + 4.0 * corner_d)
    total = jnp.pad(to_a, ((0, 1), (0, 1), (0, 0))) + jnp.pad(to_b, ((0, 1), (1, 0), (0, 0)))
    total = (
        total + jnp.pad(to_e, ((1, 0), (0, 1), (0, 0))) + jnp.pad(to_d, ((1, 0), (1, 0), (0, 0)))
    )
    return total


def contract(left, right):
    return lax.dot_general(
        left,
        right,
        (((0,), (0,)), ((), ())),
        precision=lax.Precision.HIGHEST,
        preferred_element_type=jnp.float32,
    )


def local(snapshots, region_ids, conductivity):
    strip, width = region_ids.shape
    node_rows, group_cols = snapshots.shape
    field = snapshots.reshape(strip, width, group_cols)
    weight = weights_of(region_ids, conductivity)
    below = passed_along(field[0], "mesh", -1)
    total = element_terms(field, below, weight)
    carried = passed_along(total[strip, :width], "mesh", 1)
    inner = total[:strip, :width]
    panel = jnp.concatenate([inner[:1] + carried[None], inner[1:]], 0).reshape(
        node_rows, group_cols
    )
    partial_value = contract(snapshots, lax.all_gather(panel, "snap", axis=1, tiled=True))
    summed = lax.psum_scatter(partial_value, "mesh", scatter_dimension=1, tiled=True)
    total_nodes = node_rows * lax.axis_size("mesh")
    return summed / math.sqrt(total_nodes)


def solution(mesh):
    return jax.shard_map(
        local,
        mesh=mesh,
        in_specs=(P("mesh", "snap"), P("mesh", None), P()),
        out_specs=P("snap", "mesh"),
        check_vma=False,
    )
```

profile of v0, /device:TPU:32, one launch (start us, length us, event | category | flops | bytes accessed | tf_op | source)
XLA Modules:
  0.0 477.0 jit_solution(9330290577570268332)
XLA Ops:
  6.5 0.0 all-gather.2.cloned.1.call-start
  6.5 1.0 slice.28
  7.5 1.3 collective-permute-start
  8.8 0.8 select_reduce_fusion
  9.7 1.3 collective-permute-done
  10.9 0.0 copy-start
  10.9 1.6 pad_maximum_fusion
  12.6 0.2 copy-done
  12.8 0.6 add_multiply_fusion.3
  13.5 1.3 add_multiply_fusion.2
  14.8 6.1 %collective-permute-start.1 = (f32[512,128]{1,0:T(8,128)S(1)}, f32[512,128]{1,0:T(8,128)S(1)}, u32[]{:S(2)}, u32[]{:S(2)}) collective-permute-start(f32[512,128]{1,0:T(8,128)S(1)} %add_bitcast_fusion), channel_id=1, source_target_pairs={{0,1},{1,2},{2,3},{3,4},{4,5},{5,6},{6,7},{7,8},{8,9},{9,10},{10,1... | collective-permute-start | bytes 786440 | tf_op jit(solution)/shard_map/ppermute | solution.py:11
  20.9 0.3 pad_add_fusion
  21.2 0.8 collective-permute-done.1
  22.0 0.1 add_add_fusion
  22.1 1.3 pad_maximum_fusion.1
  23.4 0.0 all-gather.2.cloned.1.call-update
  23.5 0.0 reduce-scatter.2.cloned.1.call-start
  23.5 340.8 %all-gather.2.cloned.1.call-done = f32[3072,2048]{1,0:T(8,128)} async-done(((f32[3072,128]{1,0:T(8,128)}), f32[3072,2048]{1,0:T(8,128)}) %all-gather.2.cloned.1.call-update) | async-done | bytes 25165840 | tf_op jit(solution)/shard_map/all_gather | solution.py:65
  364.4 43.1 %convolution_bitcast_fusion = f32[128,2048]{0,1:T(8,128)} fusion(f32[3072,2048]{1,0:T(8,128)} %all-gather.2.cloned.1.call-done, f32[3072,128]{1,0:T(8,128)S(1)} %copy-done), kind=kOutput, calls=%fused_computation.2 | convolution fusion | flops 9663676416 | bytes 27787264 | tf_op jit(solution)/shard_map/dot_general | solution.py:44
  407.5 0.0 reduce-scatter.2.cloned.1.call-update
  407.5 61.1 %reduce-scatter.2.cloned.1.call-done = f32[128,128]{0,1:T(8,128)} async-done(((f32[128,2048]{0,1:T(8,128)}), f32[128,128]{0,1:T(8,128)}) %reduce-scatter.2.cloned.1.call-update) | async-done | bytes 65552 | tf_op jit(solution)/shard_map/reduce_scatter | solution.py:66
  468.6 0.8 broadcast_multiply_fusion
  469.4 0.7 copy.5
  (2 shorter events, 0.0 us)
Async XLA Ops:
  6.5 357.8 %all-gather.2.cloned.1.call-start = ((), (), s32[]{:S(2)}) async-start(), calls=%async_computation.1 | async-start | bytes 26738688 | tf_op jit(solution)/shard_map/all_gather | solution.py:65
  7.5 3.4 collective-permute-start
  10.9 1.9 copy-start
  14.8 7.3 %collective-permute-start.1 = (f32[512,128]{1,0:T(8,128)S(1)}, f32[512,128]{1,0:T(8,128)S(1)}, u32[]{:S(2)}, u32[]{:S(2)}) collective-permute-start(f32[512,128]{1,0:T(8,128)S(1)} %add_bitcast_fusion), channel_id=1, source_target_pairs={{0,1},{1,2},{2,3},{3,4},{4,5},{5,6},{6,7},{7,8},{8,9},{9,10},{10,1... | collective-permute-start | bytes 786440 | tf_op jit(solution)/shard_map/ppermute | solution.py:11
  23.5 445.1 %reduce-scatter.2.cloned.1.call-start = ((), (), s32[]{:S(2)}) async-start(), calls=%async_computation.2 | async-start | bytes 1114112 | tf_op jit(solution)/shard_map/reduce_scatter | solution.py:66
Sparse Core Ops, SparseCore 0:
  23.6 340.7 all-gather.1
  407.6 60.8 reduce-scatter.1
where the time goes:
time: 477 us
  waiting for transfers between devices  404 us (85%)
  matrix products  43.1 us (9%)
  between operations  13.5 us (3%)
  starting transfers between devices  7.48 us (2%)
  other arithmetic  6.95 us (1%)
    all_gather x1, waiting for transfers between devices, local(): lax.all_gather(panel, 'snap', axis=1, tiled=True)  341 us
    reduce_scatter x1, waiting for transfers between devices, local(): lax.psum_scatter(partial_value, 'mesh', scatter_dimension=1, tiled=True)  61.1 us
    dot_general x1, matrix products, contract(): lax.dot_general(left, right, (((0,), (0,)), ((), ())), precision=lax.Prec...  43.1 us
  transfers between devices with their start and end apart: 4, of which 4 were waited for; matrix products, arithmetic and copies ran while one was open for 0% of the time, Pallas kernels for 0%

commit v1 on v0

--- a/solution.py
+++ b/solution.py
@@ -62,7 +62,18 @@
     panel = jnp.concatenate([inner[:1] + carried[None], inner[1:]], 0).reshape(
         node_rows, group_cols
     )
-    partial_value = contract(snapshots, lax.all_gather(panel, "snap", axis=1, tiled=True))
+    partial_value = contract(
+        snapshots,
+        jnp.concatenate(
+            lax.all_to_all(
+                jnp.stack([panel for _ in range(lax.axis_size("snap"))]),
+                axis_name="snap",
+                split_axis=0,
+                concat_axis=0,
+            ),
+            axis=1,
+        ),
+    )
     summed = lax.psum_scatter(partial_value, "mesh", scatter_dimension=1, tiled=True)
     total_nodes = node_rows * lax.axis_size("mesh")
     return summed / math.sqrt(total_nodes)

time: 477 us -> 687 us (1.44)
  blocking collectives: 0 us -> 556 us
  waiting for transfers between devices: 404 us -> 66.8 us
  matrix products: 43.1 us -> 20.9 us
  local copies, waits for them, and re-layouts: 1.92 us -> 16.5 us
    all_to_all x0 -> x1, blocking collectives: none -> 556 us  [local(): lax.all_to_all(jnp.stack([panel for _ in range(lax.axis_size('snap'))]),...]
    all_gather x1 -> x0, waiting for transfers between devices: 341 us -> none  [local(): lax.all_gather(panel, 'snap', axis=1, tiled=True)]
    dot_general x1, matrix products: 43.1 us -> 20.9 us  [contract(): lax.dot_general(left, right, (((0,), (0,)), ((), ())), precision=lax.Prec...]
    another operation x0 -> x2, local copies, waits for them, and re-layouts: none -> 14.6 us  [local(): jnp.stack([panel for _ in range(lax.axis_size('snap'))])]
  transfers between devices with their start and end apart: 4 -> 3, of which waited for: 4 -> 3; matrix products, arithmetic and copies ran while one was open for 0% -> 0% of each run, Pallas kernels for 0% -> 0%
where the time goes in v1:
time: 687 us
  blocking collectives  556 us (81%)
  waiting for transfers between devices  66.8 us (10%)
  matrix products  20.9 us (3%)
  local copies, waits for them, and re-layouts  16.5 us (2%)
  between operations  13.5 us (2%)
  starting transfers between devices  7.43 us (1%)
    all_to_all x1, blocking collectives, local(): lax.all_to_all(jnp.stack([panel for _ in range(lax.axis_size('snap'))]),...  556 us
    reduce_scatter x1, waiting for transfers between devices, local(): lax.psum_scatter(partial_value, 'mesh', scatter_dimension=1, tiled=True)  64.7 us
    dot_general x1, matrix products, contract(): lax.dot_general(left, right, (((0,), (0,)), ((), ())), precision=lax.Prec...  20.9 us
    another operation x2, local copies, waits for them, and re-layouts, local(): jnp.stack([panel for _ in range(lax.axis_size('snap'))])  14.6 us
  transfers between devices with their start and end apart: 3, of which 3 were waited for; matrix products, arithmetic and copies ran while one was open for 0% of the time, Pallas kernels for 0%

profile of v1, /device:TPU:32, one launch (start us, length us, event | category | flops | bytes accessed | tf_op | source)
XLA Modules:
  0.0 687.1 jit_solution(6887407007268764826)
XLA Ops:
  6.5 0.0 reduce-scatter.2.cloned.1.call-start
  6.5 1.0 slice.28
  7.5 1.3 collective-permute-start
  8.8 0.8 select_reduce_fusion
  9.7 1.3 collective-permute-done
  10.9 0.0 copy-start
  10.9 1.6 pad_maximum_fusion
  12.6 0.2 copy-done
  12.8 0.6 add_multiply_fusion.3
  13.5 1.3 add_multiply_fusion.2
  14.8 6.1 collective-permute-start.1
  20.9 0.3 pad_add_fusion
  21.2 0.8 collective-permute-done.1
  22.0 0.1 add_add_fusion
  22.1 0.1 pad_maximum_fusion.1
  22.2 1.7 copy.9
  23.9 12.9 %stack.3 = f32[16,3072,128]{1,2,0:T(8,128)} broadcast(f32[3072,128]{0,1:T(8,128)} %copy.9), dimensions={1,2} | broadcast | bytes 26738688 | tf_op jit(solution)/shard_map/stack | solution.py:69
  36.8 556.2 %all_to_all.5 = f32[16,3072,128]{1,2,0:T(8,128)S(1)} all-to-all(f32[16,3072,128]{1,2,0:T(8,128)} %stack.3), channel_id=1, replica_groups=mesh['snap'=16,'mesh'=16] {'snap'}, dimensions={0} | all-to-all | bytes 50331648 | tf_op jit(solution)/shard_map/all_to_all | solution.py:68
  593.1 20.9 %convolution_bitcast_fusion = f32[128,2048]{0,1:T(8,128)} fusion(f32[3072,2048]{0,1:T(8,128)S(1)} %bitcast.14, f32[3072,128]{1,0:T(8,128)S(1)} %copy-done), kind=kOutput, calls=%fused_computation.2 | convolution fusion | flops 9663676416 | bytes 27787264 | tf_op jit(solution)/shard_map/dot_general | solution.py:44
  614.0 0.0 reduce-scatter.2.cloned.1.call-update
  614.0 64.7 %reduce-scatter.2.cloned.1.call-done = f32[128,128]{0,1:T(8,128)} async-done(((f32[128,2048]{0,1:T(8,128)}), f32[128,128]{0,1:T(8,128)}) %reduce-scatter.2.cloned.1.call-update) | async-done | bytes 65552 | tf_op jit(solution)/shard_map/reduce_scatter | solution.py:77
  678.7 0.8 broadcast_multiply_fusion
  679.5 0.7 copy.10
  (2 shorter events, 0.0 us)
Async XLA Ops:
  6.5 672.1 %reduce-scatter.2.cloned.1.call-start = ((), (), s32[]{:S(2)}) async-start(), calls=%async_computation.2 | async-start | bytes 1114112 | tf_op jit(solution)/shard_map/reduce_scatter | solution.py:77
  7.5 3.4 collective-permute-start
  10.9 1.9 copy-start
  14.8 7.3 %collective-permute-start.1 = (f32[512,128]{1,0:T(8,128)S(1)}, f32[512,128]{1,0:T(8,128)S(1)}, u32[]{:S(2)}, u32[]{:S(2)}) collective-permute-start(f32[512,128]{1,0:T(8,128)S(1)} %add_bitcast_fusion), channel_id=1, source_target_pairs={{0,1},{1,2},{2,3},{3,4},{4,5},{5,6},{6,7},{7,8},{8,9},{9,10},{10,1... | collective-permute-start | bytes 786440 | tf_op jit(solution)/shard_map/ppermute | solution.py:11
Sparse Core Ops, SparseCore 0:
  614.1 64.4 reduce-scatter.1
